TPU v7x, 32 devices: a whole 2x2x4 slice. The times are simulated.
32 devices in a mesh: section: 4 (over x, core), mp: 8 (over z, y).
Axes of the slice: x: 2, y: 2, z: 4, core: 2. Of those that a mesh axis runs over, the one named last changes fastest.
Arguments:
- activations: bfloat16 [4, 64, 4096], P('section', 'mp'), may hold values from -24 to 24
- enc_weight: bfloat16 [4, 4096, 4096], P('section', None, 'mp'), may hold values from -0.046875 to 0.046875
- enc_bias: float32 [4096], P('mp'), may hold values from -4 to 4
- dec_weight: bfloat16 [4096, 4, 4096], P('mp', 'section'), may hold values from -2.1875 to 2.1875
- dec_bias: float32 [4, 4096], P('section'), may hold values from -3 to 3
Outputs:
- loss: float32 [], replicated
- grad_dec: bfloat16 [4096, 4, 4096], P('mp', 'section')
- grad_bias: float32 [4, 4096], P('section', 'mp')
All inputs are finite; a program needn't handle non-finite values.
Results may differ from a plain program's by a relative error of at most 0.009.
Values may be sent and summed in bfloat16 or wider, within the bound.
A program may use at most 64 MiB of HBM per device.

v0:
```python
import jax
import jax.numpy as jnp
from jax import lax
from jax.sharding import PartitionSpec as P

penalty_weight = 2.0


def local(activations, enc_weight, enc_bias, dec_weight, dec_bias):
    all_rows = lax.all_gather(activations[0], "mp", axis=0, tiled=True)
    token_count = all_rows.shape[0]
    partial_value = jnp.dot(all_rows, enc_weight[0], preferred_element_type=jnp.float32)
    w_dec = dec_weight[:, 0, :]
    layer_norm = jnp.sqrt(jnp.sum(jnp.square(w_dec.astype(jnp.float32)), axis=1) + 1e-06)
    pre_sum, norm_total = (
        lax.psum(partial_value.astype(jnp.bfloat16), "section").astype(jnp.float32),
        lax.psum(layer_norm.astype(jnp.bfloat16), "section").astype(jnp.float32),
    )
    latents = jnp.maximum(pre_sum + enc_bias[None, :], 0.0).astype(jnp.bfloat16)
    latent_float = latents.astype(jnp.float32)
    latent_sum = jnp.sum(latent_float, axis=0)
    penalty_part = penalty_weight / token_count * jnp.sum(latent_float * norm_total[None, :])
    penalty_part = jnp.where(lax.axis_index("section") == 0, penalty_part, 0.0)
    coef = penalty_weight * latent_sum / token_count / layer_norm
    col_width = w_dec.shape[1] // lax.axis_size("mp")
    first_col = lax.axis_index("mp") * col_width
    recon_t = lax.psum_scatter(
        lax.dot_general(
            w_dec, latents, (((0,), (1,)), ((), ())), preferred_element_type=jnp.float32
        ),
        "mp",
        scatter_dimension=0,
        tiled=True,
    )
    bias_cols = lax.dynamic_slice_in_dim(dec_bias[0], first_col, col_width, 0)
    x_cols = lax.dynamic_slice_in_dim(all_rows, first_col, col_width, 1)
    error_cols = recon_t + bias_cols[:, None] - x_cols.T.astype(jnp.float32)
    square_sum = jnp.sum(error_cols * error_cols)
    scaled = 2.0 * error_cols / token_count
    grad_rec_t = scaled.astype(jnp.bfloat16)
    grad_bias = jnp.sum(scaled, axis=1)[None, :]
    grad_sum = lax.dot_general(
        latents,
        lax.all_gather(grad_rec_t, "mp", axis=0, tiled=True),
        (((0,), (1,)), ((), ())),
        preferred_element_type=jnp.float32,
    )
    grad_dec = (grad_sum + coef[:, None] * w_dec.astype(jnp.float32)).astype(jnp.bfloat16)[
        :, None, :
    ]
    loss = lax.psum(square_sum / token_count + penalty_part, ("section", "mp"))
    return (loss, grad_dec, grad_bias)


def solution(mesh):
    in_specs = (
        P("section", "mp", None),
        P("section", None, "mp"),
        P("mp"),
        P("mp", "section", None),
        P("section", None),
    )
    out_specs = (P(), P("mp", "section", None), P("section", "mp"))
    return jax.shard_map(local, mesh=mesh, in_specs=in_specs, out_specs=out_specs, check_vma=False)
```

profile of v0, /device:TPU:0, one launch (start us, length us, event | category | flops | bytes accessed | tf_op | source)
XLA Modules:
  0.0 231.0 jit_solution(3103381486748929811)
XLA Ops:
  7.2 0.0 copy-start
  7.2 0.0 copy-start.2
  7.2 0.0 all-reduce.2.cloned.1.call-start
  7.2 33.2 %all-gather = bf16[1,64,4096]{2,1,0:T(8,128)(2,1)S(1)} all-gather(bf16[1,8,4096]{2,1,0:T(8,128)(2,1)} %param.5), channel_id=2, replica_groups=mesh['section'=4,'mp'=8] {'mp'}, dimensions={1}, use_global_device_ids=true | all-gather | bytes 589824 | tf_op jit(solution)/shard_map/all_gather | solution.py:10
  40.5 3.7 %fusion.7 = bf16[64,512]{1,0:T(8,128)(2,1)} fusion(bf16[1,4096,512]{2,1,0:T(8,128)(2,1)} %param.6, bf16[1,64,4096]{2,1,0:T(8,128)(2,1)S(1)} %all-gather), kind=kOutput, calls=%fused_computation.10 | convolution fusion | flops 268468224 | bytes 4784128 | tf_op jit(solution)/shard_map/dot_general | solution.py:12
  44.1 0.0 all-reduce.2.cloned.1.call-update
  44.2 0.0 reduce-scatter.2.cloned.1.call-start
  44.2 32.7 %all-reduce.2.cloned.1.call-done = bf16[64,512]{1,0:T(8,128)(2,1)} async-done(((bf16[64,512]{1,0:T(8,128)(2,1)}), bf16[64,512]{1,0:T(8,128)(2,1)}) %all-reduce.2.cloned.1.call-update) | async-done | bytes 65552 | tf_op jit(solution)/shard_map/psum | solution.py:16
  76.9 0.0 copy-done.2
  76.9 0.0 copy-start.1
  76.9 4.1 %convolution_bitcast_fusion = f32[4096,64]{0,1:T(8,128)} fusion(bf16[512,1,4096]{2,0,1:T(8,128)(2,1)} %param.8, bf16[64,512]{1,0:T(8,128)(2,1)} %all-reduce.2.cloned.1.call-done, f32[512]{0:T(512)S(1)} %copy-done.2), kind=kOutput, calls=%fused_computation.6 | convolution fusion | flops 268566528 | bytes 5310464 | tf_op jit(solution)/shard_map/dot_general | solution.py:28
  81.0 0.0 reduce-scatter.2.cloned.1.call-update
  81.1 3.1 %fusion = f32[512]{0:T(512)S(1)} fusion(bf16[512,1,4096]{2,0,1:T(8,128)(2,1)} %param.8), kind=kLoop, calls=%fused_computation.2 | loop fusion | flops 6290944 | bytes 4196352 | tf_op jit(solution)/shard_map/reduce_sum | solution.py:14
  84.1 5.8 %psum.22 = bf16[512]{0:T(512)(128)(2,1)S(1)} all-reduce(bf16[512]{0:T(512)(128)(2,1)S(1)} %sqrt_convert_fusion), channel_id=1, replica_groups=mesh['section'=4,'mp'=8] {'section'}, use_global_device_ids=true, to_apply=%region_4.0 | all-reduce | flops 512 | bytes 2048 | tf_op jit(solution)/shard_map/psum | solution.py:17
  89.9 0.0 copy-done
  89.9 0.0 copy-done.1
  89.9 0.6 convert_reduce_fusion
  91.2 54.2 %reduce-scatter.2.cloned.1.call-done = f32[512,64]{0,1:T(8,128)} async-done(((f32[4096,64]{0,1:T(8,128)}), f32[512,64]{0,1:T(8,128)}) %reduce-scatter.2.cloned.1.call-update) | async-done | bytes 131088 | tf_op jit(solution)/shard_map/reduce_scatter | solution.py:27
  145.5 1.5 multiply_reduce_fusion.1
  147.7 39.8 %psum.23 = f32[]{:T(128)} all-reduce(f32[]{:T(128)S(6)} %add.54), channel_id=1, replica_groups=mesh['section'=4,'mp'=8] {'section','mp'}, use_global_device_ids=true, to_apply=%region_6.7 | all-reduce | flops 1 | bytes 8 | tf_op jit(solution)/shard_map/psum | solution.py:51
  187.5 31.2 %all_gather.7 = bf16[4096,64]{0,1:T(8,128)(2,1)S(1)} all-gather(bf16[512,64]{0,1:T(8,128)(2,1)S(1)} %get-tuple-element.7), channel_id=1, replica_groups=mesh['section'=4,'mp'=8] {'mp'}, dimensions={0}, use_global_device_ids=true | all-gather | bytes 589824 | tf_op jit(solution)/shard_map/all_gather | solution.py:44
  218.7 5.5 %fusion.3 = bf16[512,1,4096]{2,0,1:T(8,128)(2,1)} fusion(bf16[4096,64]{0,1:T(8,128)(2,1)S(1)} %all_gather.7, bf16[512,1,4096]{2,0,1:T(8,128)(2,1)} %param.8, f32[512]{0:T(512)S(1)} %rsqrt_multiply_fusion, bf16[64,512]{1,0:T(8,128)(2,1)S(1)} %copy-done.1, f32[512]{0:T(512)S(1)} %copy-done.2), kind=kOutput, calls=%fused_computation.5 | convolution fusion | flops 276955136 | bytes 8982528 | tf_op jit(solution)/shard_map/dot_general | solution.py:42
  (4 shorter events, 0.0 us)
Async XLA Ops:
  7.2 82.8 %copy-start = (f32[1,4096]{1,0:T(1,128)S(1)}, f32[1,4096]{1,0:T(1,128)}, u32[]{:S(2)}) copy-start(f32[1,4096]{1,0:T(1,128)} %param.9) | copy-start | bytes 49156
  7.2 69.8 %copy-start.2 = (f32[512]{0:T(512)S(1)}, f32[512]{0:T(512)}, u32[]{:S(2)}) copy-start(f32[512]{0:T(512)} %param.7) | copy-start | bytes 6148
  7.2 69.8 %all-reduce.2.cloned.1.call-start = ((), (), s32[]{:S(2)}) async-start(), calls=%async_computation.1 | async-start | bytes 131072 | tf_op jit(solution)/shard_map/psum | solution.py:16
  44.2 101.3 %reduce-scatter.2.cloned.1.call-start = ((), (), s32[]{:S(2)}) async-start(), calls=%async_computation.2 | async-start | bytes 1179648 | tf_op jit(solution)/shard_map/reduce_scatter | solution.py:27
  76.9 13.0 %copy-start.1 = (bf16[64,512]{1,0:T(8,128)(2,1)S(1)}, bf16[64,512]{1,0:T(8,128)(2,1)}, u32[]{:S(2)}) copy-start(bf16[64,512]{1,0:T(8,128)(2,1)} %all-reduce.2.cloned.1.call-done) | copy-start | bytes 196612
Sparse Core Ops, SparseCore 0:
  44.3 32.6 all-reduce.1
  81.2 64.2 reduce-scatter.1
where the time goes:
time: 231 us
  blocking collectives  110 us (48%)
  waiting for transfers between devices  87 us (38%)
  between operations  15.4 us (7%)
  matrix products  13.2 us (6%)
  other arithmetic  5.29 us (2%)
    reduce_scatter x1, waiting for transfers between devices, local(): lax.psum_scatter(lax.dot_general(w_dec, latents, (((0,), (1,)), ((), ()))...  54.2 us
    psum x1, blocking collectives, local(): loss = lax.psum(square_sum / token_count + penalty_part, ('section', 'mp'))  39.8 us
    all_gather x1, blocking collectives, local(): all_rows = lax.all_gather(activations[0], 'mp', axis=0, tiled=True)  33.2 us
    psum x1, waiting for transfers between devices, local(): lax.psum(partial_value.astype(jnp.bfloat16), 'section').astype(jnp.float32)  32.7 us
    all_gather x1, blocking collectives, local(): lax.all_gather(grad_rec_t, 'mp', axis=0, tiled=True)  31.2 us
    psum x1, blocking collectives, local(): lax.psum(layer_norm.astype(jnp.bfloat16), 'section').astype(jnp.float32)  5.77 us
    dot_general x1, matrix products, local(): lax.dot_general(latents, lax.all_gather(grad_rec_t, 'mp', axis=0, tiled=T...  5.49 us
  transfers between devices with their start and end apart: 2, of which 2 were waited for; matrix products, arithmetic and copies ran while one was open for 2% of the time, Pallas kernels for 0%

commit v1 on v0

--- a/solution.py
+++ b/solution.py
@@ -48,7 +48,7 @@
     grad_dec = (grad_sum + coef[:, None] * w_dec.astype(jnp.float32)).astype(jnp.bfloat16)[
         :, None, :
     ]
-    loss = lax.psum(square_sum / token_count + penalty_part, ("section", "mp"))
+    loss = lax.psum(lax.psum(square_sum / token_count + penalty_part, "mp"), "section")
     return (loss, grad_dec, grad_bias)
 
 

time: 231 us -> 218 us (0.944)
  blocking collectives: 110 us -> 96.6 us
    psum x1 -> x2, blocking collectives: 39.8 us -> 26.1 us  [the longest x1 19.8 us: local(): lax.psum(square_sum / token_count + penalty_part, 'mp')]
where the time goes in v1:
time: 218 us
  blocking collectives  96.6 us (44%)
  waiting for transfers between devices  87 us (40%)
  between operations  15.4 us (7%)
  matrix products  13.2 us (6%)
  other arithmetic  5.29 us (2%)
    reduce_scatter x1, waiting for transfers between devices, local(): lax.psum_scatter(lax.dot_general(w_dec, latents, (((0,), (1,)), ((), ()))...  54.2 us
    all_gather x1, blocking collectives, local(): all_rows = lax.all_gather(activations[0], 'mp', axis=0, tiled=True)  33.2 us
    psum x1, waiting for transfers between devices, local(): lax.psum(partial_value.astype(jnp.bfloat16), 'section').astype(jnp.float32)  32.7 us
    all_gather x1, blocking collectives, local(): lax.all_gather(grad_rec_t, 'mp', axis=0, tiled=True)  31.5 us
    psum x1, blocking collectives, local(): lax.psum(square_sum / token_count + penalty_part, 'mp')  19.8 us
    psum x1, blocking collectives, local(): lax.psum(lax.psum(square_sum / token_count + penalty_part, 'mp'), 'section')  6.27 us
    psum x1, blocking collectives, local(): lax.psum(layer_norm.astype(jnp.bfloat16), 'section').astype(jnp.float32)  5.77 us
    dot_general x1, matrix products, local(): lax.dot_general(latents, lax.all_gather(grad_rec_t, 'mp', axis=0, tiled=T...  5.49 us
  transfers between devices with their start and end apart: 2, of which 2 were waited for; matrix products, arithmetic and copies ran while one was open for 2% of the time, Pallas kernels for 0%

profile of v1, /device:TPU:0, one launch (start us, length us, event | category | flops | bytes accessed | tf_op | source)
XLA Modules:
  0.0 217.6 jit_solution(13479778094177012924)
XLA Ops:
  7.2 0.0 copy-start
  7.2 0.0 copy-start.2
  7.2 0.0 all-reduce.2.cloned.1.call-start
  7.2 33.2 %all-gather = bf16[1,64,4096]{2,1,0:T(8,128)(2,1)S(1)} all-gather(bf16[1,8,4096]{2,1,0:T(8,128)(2,1)} %param.5), channel_id=2, replica_groups=mesh['section'=4,'mp'=8] {'mp'}, dimensions={1}, use_global_device_ids=true | all-gather | bytes 589824 | tf_op jit(solution)/shard_map/all_gather | solution.py:10
  40.5 3.7 %fusion.7 = bf16[64,512]{1,0:T(8,128)(2,1)} fusion(bf16[1,4096,512]{2,1,0:T(8,128)(2,1)} %param.6, bf16[1,64,4096]{2,1,0:T(8,128)(2,1)S(1)} %all-gather), kind=kOutput, calls=%fused_computation.10 | convolution fusion | flops 268468224 | bytes 4784128 | tf_op jit(solution)/shard_map/dot_general | solution.py:12
  44.1 0.0 all-reduce.2.cloned.1.call-update
  44.2 0.0 reduce-scatter.2.cloned.1.call-start
  44.2 32.7 %all-reduce.2.cloned.1.call-done = bf16[64,512]{1,0:T(8,128)(2,1)} async-done(((bf16[64,512]{1,0:T(8,128)(2,1)}), bf16[64,512]{1,0:T(8,128)(2,1)}) %all-reduce.2.cloned.1.call-update) | async-done | bytes 65552 | tf_op jit(solution)/shard_map/psum | solution.py:16
  76.9 0.0 copy-done.2
  76.9 0.0 copy-start.1
  76.9 4.1 %convolution_bitcast_fusion = f32[4096,64]{0,1:T(8,128)} fusion(bf16[512,1,4096]{2,0,1:T(8,128)(2,1)} %param.8, bf16[64,512]{1,0:T(8,128)(2,1)} %all-reduce.2.cloned.1.call-done, f32[512]{0:T(512)S(1)} %copy-done.2), kind=kOutput, calls=%fused_computation.6 | convolution fusion | flops 268566528 | bytes 5310464 | tf_op jit(solution)/shard_map/dot_general | solution.py:28
  81.0 0.0 reduce-scatter.2.cloned.1.call-update
  81.1 3.1 %fusion = f32[512]{0:T(512)S(1)} fusion(bf16[512,1,4096]{2,0,1:T(8,128)(2,1)} %param.8), kind=kLoop, calls=%fused_computation.2 | loop fusion | flops 6290944 | bytes 4196352 | tf_op jit(solution)/shard_map/reduce_sum | solution.py:14
  84.1 5.8 %psum.29 = bf16[512]{0:T(512)(128)(2,1)S(1)} all-reduce(bf16[512]{0:T(512)(128)(2,1)S(1)} %sqrt_convert_fusion), channel_id=1, replica_groups=mesh['section'=4,'mp'=8] {'section'}, use_global_device_ids=true, to_apply=%region_4.0 | all-reduce | flops 512 | bytes 2048 | tf_op jit(solution)/shard_map/psum | solution.py:17
  89.9 0.0 copy-done
  89.9 0.0 copy-done.1
  89.9 0.6 convert_reduce_fusion
  91.2 54.2 %reduce-scatter.2.cloned.1.call-done = f32[512,64]{0,1:T(8,128)} async-done(((f32[4096,64]{0,1:T(8,128)}), f32[512,64]{0,1:T(8,128)}) %reduce-scatter.2.cloned.1.call-update) | async-done | bytes 131088 | tf_op jit(solution)/shard_map/reduce_scatter | solution.py:27
  145.5 1.5 multiply_reduce_fusion.1
  147.7 19.8 %psum.30 = f32[]{:T(128)} all-reduce(f32[]{:T(128)S(6)} %add.56), channel_id=1, replica_groups=mesh['section'=4,'mp'=8] {'mp'}, use_global_device_ids=true, to_apply=%region_6.7 | all-reduce | flops 1 | bytes 8 | tf_op jit(solution)/shard_map/psum | solution.py:51
  167.5 6.3 %psum.31 = f32[]{:T(128)} all-reduce(f32[]{:T(128)} %psum.30), channel_id=1, replica_groups=mesh['section'=4,'mp'=8] {'section'}, use_global_device_ids=true, to_apply=%region_7.8 | all-reduce | flops 1 | bytes 8 | tf_op jit(solution)/shard_map/psum | solution.py:51
  173.8 31.5 %all_gather.7 = bf16[4096,64]{0,1:T(8,128)(2,1)S(1)} all-gather(bf16[512,64]{0,1:T(8,128)(2,1)S(1)} %get-tuple-element.7), channel_id=1, replica_groups=mesh['section'=4,'mp'=8] {'mp'}, dimensions={0}, use_global_device_ids=true | all-gather | bytes 589824 | tf_op jit(solution)/shard_map/all_gather | solution.py:44
  205.3 5.5 %fusion.3 = bf16[512,1,4096]{2,0,1:T(8,128)(2,1)} fusion(bf16[4096,64]{0,1:T(8,128)(2,1)S(1)} %all_gather.7, bf16[512,1,4096]{2,0,1:T(8,128)(2,1)} %param.8, f32[512]{0:T(512)S(1)} %rsqrt_multiply_fusion, bf16[64,512]{1,0:T(8,128)(2,1)S(1)} %copy-done.1, f32[512]{0:T(512)S(1)} %copy-done.2), kind=kOutput, calls=%fused_computation.5 | convolution fusion | flops 276955136 | bytes 8982528 | tf_op jit(solution)/shard_map/dot_general | solution.py:42
  (4 shorter events, 0.0 us)
Async XLA Ops:
  7.2 82.8 %copy-start = (f32[1,4096]{1,0:T(1,128)S(1)}, f32[1,4096]{1,0:T(1,128)}, u32[]{:S(2)}) copy-start(f32[1,4096]{1,0:T(1,128)} %param.9) | copy-start | bytes 49156
  7.2 69.8 %copy-start.2 = (f32[512]{0:T(512)S(1)}, f32[512]{0:T(512)}, u32[]{:S(2)}) copy-start(f32[512]{0:T(512)} %param.7) | copy-start | bytes 6148
  7.2 69.8 %all-reduce.2.cloned.1.call-start = ((), (), s32[]{:S(2)}) async-start(), calls=%async_computation.1 | async-start | bytes 131072 | tf_op jit(solution)/shard_map/psum | solution.py:16
  44.2 101.3 %reduce-scatter.2.cloned.1.call-start = ((), (), s32[]{:S(2)}) async-start(), calls=%async_computation.2 | async-start | bytes 1179648 | tf_op jit(solution)/shard_map/reduce_scatter | solution.py:27
  76.9 13.0 %copy-start.1 = (bf16[64,512]{1,0:T(8,128)(2,1)S(1)}, bf16[64,512]{1,0:T(8,128)(2,1)}, u32[]{:S(2)}) copy-start(bf16[64,512]{1,0:T(8,128)(2,1)} %all-reduce.2.cloned.1.call-done) | copy-start | bytes 196612
Sparse Core Ops, SparseCore 0:
  44.3 32.6 all-reduce.1
  81.2 64.2 reduce-scatter.1
